TPU v7x, 32 devices: a whole 2x2x4 slice. The times are simulated.
32 devices in a mesh: comp: 4 (over y, x), samp: 8 (over z, core).
Axes of the slice: x: 2, y: 2, z: 4, core: 2. Of those that a mesh axis runs over, the one named last changes fastest.
Arguments:
- samples: float32 [2048, 32768], P('comp', 'samp'), may hold values from -1.7 to 1.7
- unmixing: float32 [2048, 2048], P('comp', 'samp'), may hold values from -0.37565048 to 0.37565048, as said below
Outputs:
- decorrelated: float32 [2048, 2048], P('comp', 'samp')
Inputs may be any that keep to these rules, and one draw needn't show every extreme that they name: `unmixing`: every entry's magnitude is at most 17 / sqrt(2048).
All inputs are finite; a program needn't handle non-finite values.
Results may differ from a plain program's by a relative error of at most 0.00011.
Values sent between devices are 32-bit elements; how exact they have to be, the bound alone decides.
No kernel may reach another device: no remote copies, remote signals or barrier semaphores. Data moves between devices by JAX's collectives and lax.ppermute only.
A program may use at most 128 MiB of HBM per device.

v0:
```python
import jax
import jax.numpy as jnp
from jax import lax
from jax.sharding import PartitionSpec as P

NS_STEPS = 3
highest = lax.Precision.HIGHEST


def on_device(samples, unmixing):
    rows = lax.all_gather(unmixing, "samp", axis=1, tiled=True)
    whole = lax.all_gather(samples, "comp", axis=0, tiled=True)
    count = whole.shape[1] * lax.axis_size("samp")
    order = rows.shape[1]
    projected = jnp.dot(rows, whole, precision=highest)
    contrast = jnp.tanh(projected)
    slope_part = jnp.sum(1.0 - contrast * contrast, axis=1)
    moment_part = lax.dot_general(contrast, whole, (((1,), (1,)), ((), ())), precision=highest)
    moment_total, slope_total = lax.psum((moment_part, slope_part), "samp")
    updated_rows = moment_total / count - (slope_total / count)[:, None] * rows
    width = unmixing.shape[1]
    updated = lax.dynamic_slice_in_dim(updated_rows, lax.axis_index("samp") * width, width, 1)
    squares = lax.psum(jnp.sum(updated * updated), ("comp", "samp"))
    current = updated / (2.5 * jnp.sqrt(squares / order + 1e-06))
    for step in range(NS_STEPS):
        column_panel = lax.all_gather(current, "comp", axis=0, tiled=True)
        gram_part = lax.dot_general(
            current, column_panel, (((1,), (1,)), ((), ())), precision=highest
        )
        gram = lax.psum(gram_part, "samp")
        current = 1.5 * current - 0.5 * jnp.dot(gram, column_panel, precision=highest)
    return current * jnp.sqrt(jnp.float32(order))


def solution(mesh):
    return jax.shard_map(
        on_device,
        mesh=mesh,
        in_specs=(P("comp", "samp"), P("comp", "samp")),
        out_specs=P("comp", "samp"),
        check_vma=False,
    )
```

profile of v0, /device:TPU:0, one launch (start us, length us, event | category | flops | bytes accessed | tf_op | source)
XLA Modules:
  0.0 1060.8 jit_solution(8556810066995463765)
XLA Ops:
  6.5 0.0 all-gather.6.cloned.1.call-start
  6.5 0.7 all-gather.6.cloned.1.call-update
  7.3 0.0 all-gather.8.cloned.1.call-start
  7.3 0.7 all-gather.8.cloned.1.call-update
  8.0 0.0 all-reduce.5.cloned.1.call-start
  8.1 50.5 %all-gather.6.cloned.1.call-done = f32[512,2048]{1,0:T(8,128)} async-done(((f32[512,256]{1,0:T(8,128)}), f32[512,2048]{1,0:T(8,128)}) %all-gather.6.cloned.1.call-update) | async-done | bytes 4194320 | tf_op jit(solution)/shard_map/all_gather | solution.py:11
  58.6 297.8 %all-gather.8.cloned.1.call-done = f32[2048,4096]{1,0:T(8,128)} async-done(((f32[512,4096]{1,0:T(8,128)}), f32[2048,4096]{1,0:T(8,128)}) %all-gather.8.cloned.1.call-update) | async-done | bytes 33554448 | tf_op jit(solution)/shard_map/all_gather | solution.py:12
  356.3 59.6 %subtract_reduce_fusion = (f32[512]{0:T(512)S(1)}, f32[512,4096]{1,0:T(8,128)S(1)}) fusion(f32[512,2048]{1,0:T(8,128)} %all-gather.6.cloned.1.call-done, f32[2048,4096]{1,0:T(8,128)} %all-gather.8.cloned.1.call-done), kind=kOutput, calls=%fused_computation | convolution fusion | flops 51545899008 | bytes 46139392 | tf_op jit(solution)/shard_map/dot_general | solution.py:15
  415.9 58.4 %fusion = f32[512,2048]{1,0:T(8,128)} fusion(f32[2048,4096]{1,0:T(8,128)} %all-gather.8.cloned.1.call-done, f32[512,4096]{1,0:T(8,128)S(1)} %get-tuple-element.6), kind=kOutput, calls=%fused_computation.1 | convolution fusion | flops 51539607552 | bytes 46137344 | tf_op jit(solution)/shard_map/dot_general | solution.py:18
  474.3 0.0 all-reduce.5.cloned.1.call-update
  474.3 0.0 all-gather.10.cloned.1.call-start
  474.4 16.7 %psum.43 = f32[512]{0:T(512)S(1)} all-reduce(f32[512]{0:T(512)S(1)} %get-tuple-element.5), channel_id=1, replica_groups=mesh['comp'=4,'samp'=8] {'samp'}, use_global_device_ids=true, to_apply=%region_2.0 | all-reduce | flops 512 | bytes 4096 | tf_op jit(solution)/shard_map/psum | solution.py:19
  491.1 80.0 %all-reduce.5.cloned.1.call-done = f32[512,2048]{1,0:T(8,128)} async-done(((f32[512,2048]{1,0:T(8,128)}), f32[512,2048]{1,0:T(8,128)}) %all-reduce.5.cloned.1.call-update) | async-done | bytes 4194320 | tf_op jit(solution)/shard_map/psum | solution.py:19
  571.1 2.0 multiply_reduce_fusion
  573.1 40.4 %psum.44 = f32[]{:T(128)} all-reduce(f32[]{:T(128)} %multiply_reduce_fusion), channel_id=1, replica_groups=mesh['comp'=4,'samp'=8] {'comp','samp'}, use_global_device_ids=true, to_apply=%region_4.0 | all-reduce | flops 1 | bytes 8 | tf_op jit(solution)/shard_map/psum | solution.py:23
  614.2 2.1 broadcast_divide_fusion
  616.4 0.0 all-gather.10.cloned.1.call-update
  616.4 0.0 copy-start.5
  616.4 0.2 all-reduce.7.cloned.1.call-start
  616.7 35.0 %all-gather.10.cloned.1.call-done = f32[2048,256]{1,0:T(8,128)} async-done(((f32[512,256]{1,0:T(8,128)}), f32[2048,256]{1,0:T(8,128)}) %all-gather.10.cloned.1.call-update) | async-done | bytes 2097168 | tf_op jit(solution)/shard_map/all_gather | solution.py:26
  651.7 7.4 fusion.7
  659.1 0.0 all-reduce.7.cloned.1.call-update
  659.1 0.0 all-gather.12.cloned.1.call-start
  659.2 96.6 %all-reduce.7.cloned.1.call-done = f32[512,2048]{1,0:T(8,128)} async-done(((f32[512,2048]{1,0:T(8,128)}), f32[512,2048]{1,0:T(8,128)}) %all-reduce.7.cloned.1.call-update) | async-done | bytes 4194320 | tf_op jit(solution)/shard_map/psum | solution.py:30
  755.8 0.0 copy-done.5
  755.8 0.0 copy-done.2
  755.8 6.4 fusion.5
  762.2 0.0 all-gather.12.cloned.1.call-update
  762.2 0.0 copy-start
  762.2 0.0 all-reduce.9.cloned.1.call-start
  762.3 35.3 %all-gather.12.cloned.1.call-done = f32[2048,256]{1,0:T(8,128)} async-done(((f32[512,256]{1,0:T(8,128)}), f32[2048,256]{1,0:T(8,128)}) %all-gather.12.cloned.1.call-update) | async-done | bytes 2097168 | tf_op jit(solution)/shard_map/all_gather | solution.py:26
  797.6 7.4 fusion.8
  805.0 0.0 all-reduce.9.cloned.1.call-update
  805.0 0.3 all-gather.14.cloned.1.call-start
  805.3 96.4 %all-reduce.9.cloned.1.call-done = f32[512,2048]{1,0:T(8,128)} async-done(((f32[512,2048]{1,0:T(8,128)}), f32[512,2048]{1,0:T(8,128)}) %all-reduce.9.cloned.1.call-update) | async-done | bytes 4194320 | tf_op jit(solution)/shard_map/psum | solution.py:30
  901.7 0.0 copy-done
  901.7 0.0 copy-done.3
  901.7 6.4 fusion.4
  908.1 0.0 all-gather.14.cloned.1.call-update
  908.1 0.0 copy-start.1
  908.2 0.0 all-reduce.11.cloned.1.call-start
  908.2 35.3 %all-gather.14.cloned.1.call-done = f32[2048,256]{1,0:T(8,128)} async-done(((f32[512,256]{1,0:T(8,128)}), f32[2048,256]{1,0:T(8,128)}) %all-gather.14.cloned.1.call-update) | async-done | bytes 2097168 | tf_op jit(solution)/shard_map/all_gather | solution.py:26
  943.5 7.4 fusion.9
  950.9 0.0 all-reduce.11.cloned.1.call-update
  951.0 96.6 %all-reduce.11.cloned.1.call-done = f32[512,2048]{1,0:T(8,128)} async-done(((f32[512,2048]{1,0:T(8,128)}), f32[512,2048]{1,0:T(8,128)}) %all-reduce.11.cloned.1.call-update) | async-done | bytes 4194320 | tf_op jit(solution)/shard_map/psum | solution.py:30
  1047.6 0.0 copy-done.1
  1047.6 0.0 copy-done.4
  1047.6 6.4 fusion.3
  (4 shorter events, 0.0 us)
Async XLA Ops:
  6.5 52.0 %all-gather.6.cloned.1.call-start = ((), (), s32[]{:S(2)}) async-start(), calls=%async_computation | async-start | bytes 4718592 | tf_op jit(solution)/shard_map/all_gather | solution.py:11
  7.3 349.1 %all-gather.8.cloned.1.call-start = ((), (), s32[]{:S(2)}) async-start(), calls=%async_computation.1 | async-start | bytes 41943040 | tf_op jit(solution)/shard_map/all_gather | solution.py:12
  8.0 563.1 %all-reduce.5.cloned.1.call-start = ((), (), s32[]{:S(2)}) async-start(), calls=%async_computation.2 | async-start | bytes 8388608 | tf_op jit(solution)/shard_map/psum | solution.py:19
  474.3 177.4 %all-gather.10.cloned.1.call-start = ((), (), s32[]{:S(2)}) async-start(), calls=%async_computation.3 | async-start | bytes 2621440 | tf_op jit(solution)/shard_map/all_gather | solution.py:26
  616.4 139.4 %copy-start.5 = (f32[512,256]{1,0:T(8,128)S(1)}, f32[512,256]{1,0:T(8,128)}, u32[]{:S(2)}) copy-start(f32[512,256]{1,0:T(8,128)} %broadcast_divide_fusion) | copy-start | bytes 1572868
  616.4 139.3 %all-reduce.7.cloned.1.call-start = ((), (), s32[]{:S(2)}) async-start(), calls=%async_computation.4 | async-start | bytes 8388608 | tf_op jit(solution)/shard_map/psum | solution.py:30
  651.7 104.1 %copy-start.2 = (f32[2048,256]{1,0:T(8,128)S(1)}, f32[2048,256]{1,0:T(8,128)}, u32[]{:S(2)}) copy-start(f32[2048,256]{1,0:T(8,128)} %all-gather.10.cloned.1.call-done) | copy-start | bytes 6291460
  659.1 138.5 %all-gather.12.cloned.1.call-start = ((), (), s32[]{:S(2)}) async-start(), calls=%async_computation.5 | async-start | bytes 2621440 | tf_op jit(solution)/shard_map/all_gather | solution.py:26
  762.2 139.5 %copy-start = (f32[512,256]{1,0:T(8,128)S(1)}, f32[512,256]{1,0:T(8,128)}, u32[]{:S(2)}) copy-start(f32[512,256]{1,0:T(8,128)} %fusion.5) | copy-start | bytes 1572868
  762.2 139.4 %all-reduce.9.cloned.1.call-start = ((), (), s32[]{:S(2)}) async-start(), calls=%async_computation.6 | async-start | bytes 8388608 | tf_op jit(solution)/shard_map/psum | solution.py:30
  797.6 104.1 %copy-start.3 = (f32[2048,256]{1,0:T(8,128)S(1)}, f32[2048,256]{1,0:T(8,128)}, u32[]{:S(2)}) copy-start(f32[2048,256]{1,0:T(8,128)} %all-gather.12.cloned.1.call-done) | copy-start | bytes 6291460
  805.0 138.5 %all-gather.14.cloned.1.call-start = ((), (), s32[]{:S(2)}) async-start(), calls=%async_computation.7 | async-start | bytes 2621440 | tf_op jit(solution)/shard_map/all_gather | solution.py:26
  908.1 139.5 %copy-start.1 = (f32[512,256]{1,0:T(8,128)S(1)}, f32[512,256]{1,0:T(8,128)}, u32[]{:S(2)}) copy-start(f32[512,256]{1,0:T(8,128)} %fusion.4) | copy-start | bytes 1572868
  908.2 139.4 %all-reduce.11.cloned.1.call-start = ((), (), s32[]{:S(2)}) async-start(), calls=%async_computation.8 | async-start | bytes 8388608 | tf_op jit(solution)/shard_map/psum | solution.py:30
  943.5 104.1 %copy-start.4 = (f32[2048,256]{1,0:T(8,128)S(1)}, f32[2048,256]{1,0:T(8,128)}, u32[]{:S(2)}) copy-start(f32[2048,256]{1,0:T(8,128)} %all-gather.14.cloned.1.call-done) | copy-start | bytes 6291460
Sparse Core Ops, SparseCore 0:
  8.9 49.5 all-gather.5
  60.4 295.8 all-gather.7
  474.4 96.6 all-reduce.4
  616.5 35.1 all-gather.9
  659.3 96.4 all-reduce.6
  762.3 35.2 all-gather.11
  805.2 96.4 all-reduce.8
  908.3 35.2 all-gather.13
  951.1 96.4 all-reduce.10
where the time goes:
time: 1070 us; the launch traced here: 1060 us
  waiting for transfers between devices  825 us (77%)
  matrix products  159 us (15%)
  blocking collectives  57.1 us (5%)
  between operations  14.2 us (1%)
    all_gather x1, waiting for transfers between devices, on_device(): whole = lax.all_gather(samples, 'comp', axis=0, tiled=True)  298 us
    psum x3, waiting for transfers between devices, on_device(): gram = lax.psum(gram_part, 'samp')  290 us
    all_gather x3, waiting for transfers between devices, on_device(): column_panel = lax.all_gather(current, 'comp', axis=0, tiled=True)  106 us
    psum x1, waiting for transfers between devices, on_device(): moment_total, slope_total = lax.psum((moment_part, slope_part), 'samp')  80 us
    dot_general x1, matrix products, on_device(): projected = jnp.dot(rows, whole, precision=highest)  59.6 us
    dot_general x1, matrix products, on_device(): lax.dot_general(contrast, whole, (((1,), (1,)), ((), ())), precision=high...  58.4 us
    all_gather x1, waiting for transfers between devices, on_device(): rows = lax.all_gather(unmixing, 'samp', axis=1, tiled=True)  50.5 us
    psum x1, blocking collectives, on_device(): squares = lax.psum(jnp.sum(updated * updated), ('comp', 'samp'))  40.4 us
  transfers between devices with their start and end apart: 9, of which 9 were waited for; matrix products, arithmetic and copies ran while one was open for 0% of the time, Pallas kernels for 0%

commit v1 on v0

--- a/solution.py
+++ b/solution.py
@@ -27,7 +27,10 @@
         gram_part = lax.dot_general(
             current, column_panel, (((1,), (1,)), ((), ())), precision=highest
         )
-        gram = lax.psum(gram_part, "samp")
+        peers, gram = (lax.axis_size("samp"), gram_part)
+        for stride in [1 << k for k in range(peers.bit_length() - 1)]:
+            route = [(i, i ^ stride) for i in range(peers)]
+            gram = gram + lax.ppermute(gram, "samp", route)
         current = 1.5 * current - 0.5 * jnp.dot(gram, column_panel, precision=highest)
     return current * jnp.sqrt(jnp.float32(order))
 

time: 1070 us -> 1620 us (1.51)
  waiting for transfers between devices: 825 us -> 1370 us
    ppermute x0 -> x9, waiting for transfers between devices: none -> 835 us  [on_device(): gram = gram + lax.ppermute(gram, 'samp', route)]
    psum x3 -> x0, waiting for transfers between devices: 290 us -> none  [on_device(): gram = lax.psum(gram_part, 'samp')]
  transfers between devices with their start and end apart: 9 -> 15, of which waited for: 9 -> 15; matrix products, arithmetic and copies ran while one was open for 0% -> 0% of each run, Pallas kernels for 0% -> 0%
where the time goes in v1:
time: 1620 us; the launch traced here: 1610 us
  waiting for transfers between devices  1370 us (85%)
  matrix products  148 us (9%)
  blocking collectives  57.1 us (4%)
    ppermute x9, waiting for transfers between devices, on_device(): gram = gram + lax.ppermute(gram, 'samp', route)  835 us
    all_gather x1, waiting for transfers between devices, on_device(): whole = lax.all_gather(samples, 'comp', axis=0, tiled=True)  298 us
    all_gather x3, waiting for transfers between devices, on_device(): column_panel = lax.all_gather(current, 'comp', axis=0, tiled=True)  105 us
    psum x1, waiting for transfers between devices, on_device(): moment_total, slope_total = lax.psum((moment_part, slope_part), 'samp')  80 us
    dot_general x1, matrix products, on_device(): projected = jnp.dot(rows, whole, precision=highest)  59.6 us
    dot_general x1, matrix products, on_device(): lax.dot_general(contrast, whole, (((1,), (1,)), ((), ())), precision=high...  58.2 us
    all_gather x1, waiting for transfers between devices, on_device(): rows = lax.all_gather(unmixing, 'samp', axis=1, tiled=True)  50.5 us
    psum x1, blocking collectives, on_device(): squares = lax.psum(jnp.sum(updated * updated), ('comp', 'samp'))  40.4 us
  transfers between devices with their start and end apart: 15, of which 15 were waited for; matrix products, arithmetic and copies ran while one was open for 0% of the time, Pallas kernels for 0%

profile of v1, /device:TPU:0, one launch (start us, length us, event | category | flops | bytes accessed | tf_op | source)
XLA Modules:
  0.0 1613.2 jit_solution(12703637321558952436)
XLA Ops:
  6.5 0.7 all-gather.6.cloned.1.call-update
  7.3 0.7 all-gather.8.cloned.1.call-update
  8.0 0.0 all-reduce.2.cloned.1.call-start
  8.1 50.5 %all-gather.6.cloned.1.call-done = f32[512,2048]{1,0:T(8,128)} async-done(((f32[512,256]{1,0:T(8,128)}), f32[512,2048]{1,0:T(8,128)}) %all-gather.6.cloned.1.call-update) | async-done | bytes 4194320 | tf_op jit(solution)/shard_map/all_gather | solution.py:11
  58.6 297.8 %all-gather.8.cloned.1.call-done = f32[2048,4096]{1,0:T(8,128)} async-done(((f32[512,4096]{1,0:T(8,128)}), f32[2048,4096]{1,0:T(8,128)}) %all-gather.8.cloned.1.call-update) | async-done | bytes 33554448 | tf_op jit(solution)/shard_map/all_gather | solution.py:12
  356.3 59.6 %subtract_reduce_fusion = (f32[512]{0:T(512)S(1)}, f32[512,4096]{1,0:T(8,128)S(1)}) fusion(f32[512,2048]{1,0:T(8,128)} %all-gather.6.cloned.1.call-done, f32[2048,4096]{1,0:T(8,128)} %all-gather.8.cloned.1.call-done), kind=kOutput, calls=%fused_computation | convolution fusion | flops 51545899008 | bytes 46139392 | tf_op jit(solution)/shard_map/dot_general | solution.py:15
  415.9 58.2 %fusion = f32[512,2048]{1,0:T(8,128)} fusion(f32[2048,4096]{1,0:T(8,128)} %all-gather.8.cloned.1.call-done, f32[512,4096]{1,0:T(8,128)S(1)} %get-tuple-element.6), kind=kOutput, calls=%fused_computation.1 | convolution fusion | flops 51539607552 | bytes 46137344 | tf_op jit(solution)/shard_map/dot_general | solution.py:18
  474.1 0.0 all-gather.10.cloned.1.call-start
  474.1 16.7 %psum.22 = f32[512]{0:T(512)S(1)} all-reduce(f32[512]{0:T(512)S(1)} %get-tuple-element.5), channel_id=1, replica_groups=mesh['comp'=4,'samp'=8] {'samp'}, use_global_device_ids=true, to_apply=%region_2.0 | all-reduce | flops 512 | bytes 4096 | tf_op jit(solution)/shard_map/psum | solution.py:19
  490.9 80.0 %all-reduce.2.cloned.1.call-done = f32[512,2048]{1,0:T(8,128)} async-done(((f32[512,2048]{1,0:T(8,128)}), f32[512,2048]{1,0:T(8,128)}) %all-reduce.2.cloned.1.call-update) | async-done | bytes 4194320 | tf_op jit(solution)/shard_map/psum | solution.py:19
  570.9 2.0 multiply_reduce_fusion
  572.9 40.4 %psum.23 = f32[]{:T(128)} all-reduce(f32[]{:T(128)} %multiply_reduce_fusion), channel_id=1, replica_groups=mesh['comp'=4,'samp'=8] {'comp','samp'}, use_global_device_ids=true, to_apply=%region_4.0 | all-reduce | flops 1 | bytes 8 | tf_op jit(solution)/shard_map/psum | solution.py:23
  614.0 2.1 broadcast_divide_fusion
  616.2 0.3 all-gather.12.cloned.1.call-start
  616.5 35.0 %all-gather.10.cloned.1.call-done = f32[2048,256]{1,0:T(8,128)} async-done(((f32[512,256]{1,0:T(8,128)}), f32[2048,256]{1,0:T(8,128)}) %all-gather.10.cloned.1.call-update) | async-done | bytes 2097168 | tf_op jit(solution)/shard_map/all_gather | solution.py:26
  651.5 5.6 fusion.25
  657.1 0.1 collective-permute-start
  657.2 7.1 collective-permute-done
  664.3 1.1 add.41
  665.4 1.6 collective-permute-start.1
  667.0 91.1 %collective-permute-done.1 = f32[512,2048]{1,0:T(8,128)S(1)} collective-permute-done((f32[512,2048]{1,0:T(8,128)S(1)}, f32[512,2048]{1,0:T(8,128)S(1)}, u32[]{:S(2)}, u32[]{:S(2)}) %collective-permute-start.1) | collective-permute-done | bytes 4194336 | tf_op jit(solution)/shard_map/ppermute | solution.py:33
  758.1 1.1 add.42
  759.2 2.5 collective-permute-start.2
  761.7 180.1 %collective-permute-done.2 = f32[512,2048]{1,0:T(8,128)S(1)} collective-permute-done((f32[512,2048]{1,0:T(8,128)S(1)}, f32[512,2048]{1,0:T(8,128)S(1)}, u32[]{:S(2)}, u32[]{:S(2)}) %collective-permute-start.2) | collective-permute-done | bytes 4194336 | tf_op jit(solution)/shard_map/ppermute | solution.py:33
  941.8 4.3 fusion.17
  946.1 0.4 all-gather.14.cloned.1.call-start
  946.6 34.9 %all-gather.12.cloned.1.call-done = f32[2048,256]{1,0:T(8,128)} async-done(((f32[512,256]{1,0:T(8,128)}), f32[2048,256]{1,0:T(8,128)}) %all-gather.12.cloned.1.call-update) | async-done | bytes 2097168 | tf_op jit(solution)/shard_map/all_gather | solution.py:26
  981.4 5.6 fusion.26
  987.1 0.1 collective-permute-start.3
  987.1 7.1 collective-permute-done.3
  994.3 1.1 add.44
  995.4 1.6 collective-permute-start.4
  996.9 91.1 %collective-permute-done.4 = f32[512,2048]{1,0:T(8,128)S(1)} collective-permute-done((f32[512,2048]{1,0:T(8,128)S(1)}, f32[512,2048]{1,0:T(8,128)S(1)}, u32[]{:S(2)}, u32[]{:S(2)}) %collective-permute-start.4) | collective-permute-done | bytes 4194336 | tf_op jit(solution)/shard_map/ppermute | solution.py:33
  1088.1 1.1 add.45
  1089.2 2.5 collective-permute-start.5
  1091.6 180.1 %collective-permute-done.5 = f32[512,2048]{1,0:T(8,128)S(1)} collective-permute-done((f32[512,2048]{1,0:T(8,128)S(1)}, f32[512,2048]{1,0:T(8,128)S(1)}, u32[]{:S(2)}, u32[]{:S(2)}) %collective-permute-start.5) | collective-permute-done | bytes 4194336 | tf_op jit(solution)/shard_map/ppermute | solution.py:33
  1271.8 4.3 multiply_subtract_fusion
  1276.1 35.3 %all-gather.14.cloned.1.call-done = f32[2048,256]{1,0:T(8,128)} async-done(((f32[512,256]{1,0:T(8,128)}), f32[2048,256]{1,0:T(8,128)}) %all-gather.14.cloned.1.call-update) | async-done | bytes 2097168 | tf_op jit(solution)/shard_map/all_gather | solution.py:26
  1311.4 5.8 fusion.27
  1317.2 0.1 collective-permute-start.6
  1317.3 7.1 collective-permute-done.6
  1324.4 1.1 add.47
  1325.5 1.6 collective-permute-start.7
  1327.1 91.1 %collective-permute-done.7 = f32[512,2048]{1,0:T(8,128)S(1)} collective-permute-done((f32[512,2048]{1,0:T(8,128)S(1)}, f32[512,2048]{1,0:T(8,128)S(1)}, u32[]{:S(2)}, u32[]{:S(2)}) %collective-permute-start.7) | collective-permute-done | bytes 4194336 | tf_op jit(solution)/shard_map/ppermute | solution.py:33
  1418.2 1.1 add.48
  1419.3 2.5 collective-permute-start.8
  1421.8 180.1 %collective-permute-done.8 = f32[512,2048]{1,0:T(8,128)S(1)} collective-permute-done((f32[512,2048]{1,0:T(8,128)S(1)}, f32[512,2048]{1,0:T(8,128)S(1)}, u32[]{:S(2)}, u32[]{:S(2)}) %collective-permute-start.8) | collective-permute-done | bytes 4194336 | tf_op jit(solution)/shard_map/ppermute | solution.py:33
  1601.9 4.3 subtract_multiply_fusion
  (19 shorter events, 0.1 us)
Async XLA Ops:
  6.5 52.0 %all-gather.6.cloned.1.call-start = ((), (), s32[]{:S(2)}) async-start(), calls=%async_computation | async-start | bytes 4718592 | tf_op jit(solution)/shard_map/all_gather | solution.py:11
  7.3 349.1 %all-gather.8.cloned.1.call-start = ((), (), s32[]{:S(2)}) async-start(), calls=%async_computation.1 | async-start | bytes 41943040 | tf_op jit(solution)/shard_map/all_gather | solution.py:12
  8.0 562.9 %all-reduce.2.cloned.1.call-start = ((), (), s32[]{:S(2)}) async-start(), calls=%async_computation.2 | async-start | bytes 8388608 | tf_op jit(solution)/shard_map/psum | solution.py:19
  474.1 177.4 %all-gather.10.cloned.1.call-start = ((), (), s32[]{:S(2)}) async-start(), calls=%async_computation.3 | async-start | bytes 2621440 | tf_op jit(solution)/shard_map/all_gather | solution.py:26
  616.2 365.2 %all-gather.12.cloned.1.call-start = ((), (), s32[]{:S(2)}) async-start(), calls=%async_computation.4 | async-start | bytes 2621440 | tf_op jit(solution)/shard_map/all_gather | solution.py:26
  657.1 7.2 collective-permute-start
  665.4 276.4 %copy-start.2 = (f32[2048,256]{1,0:T(8,128)S(1)}, f32[2048,256]{1,0:T(8,128)}, u32[]{:S(2)}) copy-start(f32[2048,256]{1,0:T(8,128)} %all-gather.10.cloned.1.call-done) | copy-start | bytes 6291460
  665.4 276.4 %copy-start.5 = (f32[512,256]{1,0:T(8,128)S(1)}, f32[512,256]{1,0:T(8,128)}, u32[]{:S(2)}) copy-start(f32[512,256]{1,0:T(8,128)} %broadcast_divide_fusion) | copy-start | bytes 1572868
  665.4 92.7 %collective-permute-start.1 = (f32[512,2048]{1,0:T(8,128)S(1)}, f32[512,2048]{1,0:T(8,128)S(1)}, u32[]{:S(2)}, u32[]{:S(2)}) collective-permute-start(f32[512,2048]{1,0:T(8,128)S(1)} %add.41), channel_id=1, source_target_pairs={{0,2},{1,3},{2,0},{3,1},{4,6},{5,7},{6,4},{7,5},{8,10},{9,11},{10,... | collective-permute-start | bytes 12582920 | tf_op jit(solution)/shard_map/ppermute | solution.py:33
  759.2 182.6 %collective-permute-start.2 = (f32[512,2048]{1,0:T(8,128)S(1)}, f32[512,2048]{1,0:T(8,128)S(1)}, u32[]{:S(2)}, u32[]{:S(2)}) collective-permute-start(f32[512,2048]{1,0:T(8,128)S(1)} %add.42), channel_id=1, source_target_pairs={{0,4},{1,5},{2,6},{3,7},{4,0},{5,1},{6,2},{7,3},{8,12},{9,13},{10,... | collective-permute-start | bytes 12582920 | tf_op jit(solution)/shard_map/ppermute | solution.py:33
  946.1 365.3 %all-gather.14.cloned.1.call-start = ((), (), s32[]{:S(2)}) async-start(), calls=%async_computation.5 | async-start | bytes 2621440 | tf_op jit(solution)/shard_map/all_gather | solution.py:26
  987.1 7.2 collective-permute-start.3
  995.4 276.4 %copy-start = (f32[512,256]{1,0:T(8,128)S(1)}, f32[512,256]{1,0:T(8,128)}, u32[]{:S(2)}) copy-start(f32[512,256]{1,0:T(8,128)} %fusion.17) | copy-start | bytes 1572868
  995.4 276.4 %copy-start.3 = (f32[2048,256]{1,0:T(8,128)S(1)}, f32[2048,256]{1,0:T(8,128)}, u32[]{:S(2)}) copy-start(f32[2048,256]{1,0:T(8,128)} %all-gather.12.cloned.1.call-done) | copy-start | bytes 6291460
  995.4 92.7 %collective-permute-start.4 = (f32[512,2048]{1,0:T(8,128)S(1)}, f32[512,2048]{1,0:T(8,128)S(1)}, u32[]{:S(2)}, u32[]{:S(2)}) collective-permute-start(f32[512,2048]{1,0:T(8,128)S(1)} %add.44), channel_id=1, source_target_pairs={{0,2},{1,3},{2,0},{3,1},{4,6},{5,7},{6,4},{7,5},{8,10},{9,11},{10,... | collective-permute-start | bytes 12582920 | tf_op jit(solution)/shard_map/ppermute | solution.py:33
  1089.2 182.6 %collective-permute-start.5 = (f32[512,2048]{1,0:T(8,128)S(1)}, f32[512,2048]{1,0:T(8,128)S(1)}, u32[]{:S(2)}, u32[]{:S(2)}) collective-permute-start(f32[512,2048]{1,0:T(8,128)S(1)} %add.45), channel_id=1, source_target_pairs={{0,4},{1,5},{2,6},{3,7},{4,0},{5,1},{6,2},{7,3},{8,12},{9,13},{10,... | collective-permute-start | bytes 12582920 | tf_op jit(solution)/shard_map/ppermute | solution.py:33
  1317.2 7.2 collective-permute-start.6
  1325.5 276.4 %copy-start.1 = (f32[512,256]{1,0:T(8,128)S(1)}, f32[512,256]{1,0:T(8,128)}, u32[]{:S(2)}) copy-start(f32[512,256]{1,0:T(8,128)} %multiply_subtract_fusion) | copy-start | bytes 1572868
  1325.5 276.4 %copy-start.4 = (f32[2048,256]{1,0:T(8,128)S(1)}, f32[2048,256]{1,0:T(8,128)}, u32[]{:S(2)}) copy-start(f32[2048,256]{1,0:T(8,128)} %all-gather.14.cloned.1.call-done) | copy-start | bytes 6291460
  1325.5 92.7 %collective-permute-start.7 = (f32[512,2048]{1,0:T(8,128)S(1)}, f32[512,2048]{1,0:T(8,128)S(1)}, u32[]{:S(2)}, u32[]{:S(2)}) collective-permute-start(f32[512,2048]{1,0:T(8,128)S(1)} %add.47), channel_id=1, source_target_pairs={{0,2},{1,3},{2,0},{3,1},{4,6},{5,7},{6,4},{7,5},{8,10},{9,11},{10,... | collective-permute-start | bytes 12582920 | tf_op jit(solution)/shard_map/ppermute | solution.py:33
  1419.3 182.6 %collective-permute-start.8 = (f32[512,2048]{1,0:T(8,128)S(1)}, f32[512,2048]{1,0:T(8,128)S(1)}, u32[]{:S(2)}, u32[]{:S(2)}) collective-permute-start(f32[512,2048]{1,0:T(8,128)S(1)} %add.48), channel_id=1, source_target_pairs={{0,4},{1,5},{2,6},{3,7},{4,0},{5,1},{6,2},{7,3},{8,12},{9,13},{10,... | collective-permute-start | bytes 12582920 | tf_op jit(solution)/shard_map/ppermute | solution.py:33
Sparse Core Ops, SparseCore 0:
  8.9 49.5 all-gather.5
  60.4 295.8 all-gather.7
  474.2 96.6 all-reduce.1
  616.3 35.1 all-gather.9
  946.2 35.1 all-gather.11
  1276.2 35.1 all-gather.13
